TPU v7x, 32 devices: a whole 2x2x4 slice. The times are simulated.
32 devices in a mesh: groups: 2 (over y), seq: 4 (over z), head: 2 (over x), rep: 2 (over core).
Axes of the slice: x: 2, y: 2, z: 4, core: 2. Of those that a mesh axis runs over, the one named last changes fastest.
Arguments:
- queries: bfloat16 [8192, 4096], P(('groups', 'seq', 'rep'), 'head'), parts along dimension 0, may hold values from -6 to 6
- keys: bfloat16 [8192, 4096], P(('groups', 'seq', 'rep'), 'head'), parts along dimension 0, may hold values from -6 to 6
- values: bfloat16 [8192, 4096], P(('groups', 'seq', 'rep'), 'head'), parts along dimension 0, may hold values from -6 to 6
- d_out: bfloat16 [8192, 4096], P(('groups', 'seq', 'rep'), 'head'), parts along dimension 0, may hold values from -6 to 6
- doc_lengths: int32 [16], P('groups'), parts along dimension 0, may hold values from 1 to 2048, 4096 in all
- gain: float32 [4096], P('head'), may hold values from 0.25 to 1.75
Outputs:
- mixed: bfloat16 [8192, 4096], P(('groups', 'seq', 'rep'), 'head'), parts along dimension 0
- grad_queries: bfloat16 [8192, 4096], P(('groups', 'seq', 'rep'), 'head'), parts along dimension 0
- grad_keys: bfloat16 [8192, 4096], P(('groups', 'seq', 'rep'), 'head'), parts along dimension 0
- grad_values: bfloat16 [8192, 4096], P(('groups', 'seq', 'rep'), 'head'), parts along dimension 0
- grad_gain: float32 [2, 4096], P('groups', 'head'), parts along dimension 0
There are 2 independent parts, one for each index of `groups`. A program takes and returns all parts, laid end to end along the dimension named above; an argument that names none is the same for every part. Nothing has to cross between parts.
Inputs may be any that keep to these rules, and one draw needn't show every extreme that they name: `doc_lengths`: the entries sum to 4096, and the largest is exactly half of 4096.
All inputs are finite; a program needn't handle non-finite values.
Results may differ from a plain program's by a relative error of at most 0.0059.
Values sent between devices are 32-bit elements; how exact they have to be, the bound alone decides.
A program may use at most 128 MiB of HBM per device.

v0:
```python
import math

import jax
import jax.numpy as jnp
from jax import lax
from jax.sharding import PartitionSpec as P

DH = 128
BLOCK = 512


def prefix(value, axis, join, neutral, backward):
    count, mine = (lax.axis_size(axis), lax.axis_index(axis))
    pieces = jax.tree.map(lambda part: lax.all_gather(part, axis), value)
    if backward:
        pieces = jax.tree.map(lambda part: part[::-1], pieces)
        mine = count - 1 - mine
    subtotal = jax.tree.map(
        lambda part, zero: jnp.full_like(part, 0) + jnp.asarray(zero, part.dtype), value, neutral
    )

    def hop(position, subtotal):
        longer = join(subtotal, jax.tree.map(lambda part: part[position], pieces))
        return jax.tree.map(lambda new, old: jnp.where(position < mine, new, old), longer, subtotal)

    return lax.fori_loop(0, count - 1, hop, subtotal)


def doc_index(doc_ends, places):
    return jnp.sum((doc_ends[None, :] <= places[:, None]).astype(jnp.int32), axis=1)


def carry_state(earlier, latter):
    return (latter[0] + (1.0 - latter[1][0]) * earlier[0], jnp.maximum(earlier[1], latter[1]))


def same_doc(block_docs):
    places = jnp.arange(block_docs.shape[0])
    return (block_docs[:, None] == block_docs[None, :]) & (places[:, None] >= places[None, :])


def forward_block(state_in, inputs):
    query_blk, key_blk, value_blk, block_docs, prior_doc = inputs
    scores = jnp.einsum("thd,shd->hts", query_blk, key_blk, preferred_element_type=jnp.float32) / DH
    weights = jnp.where(same_doc(block_docs)[None], scores, 0.0).astype(jnp.bfloat16)
    inner_sum = jnp.einsum("hts,shd->thd", weights, value_blk, preferred_element_type=jnp.float32)
    carried = (
        jnp.einsum(
            "thd,hde->the",
            query_blk,
            state_in.astype(jnp.bfloat16),
            preferred_element_type=jnp.float32,
        )
        / DH
    )
    output = inner_sum + jnp.where((block_docs == prior_doc)[:, None, None], carried, 0.0)
    tail_mask = (block_docs == block_docs[-1]).astype(jnp.bfloat16)
    local_sum = jnp.einsum(
        "thd,the->hde",
        key_blk * tail_mask[:, None, None],
        value_blk,
        preferred_element_type=jnp.float32,
    )
    renewed = local_sum + jnp.where(block_docs[-1] == prior_doc, state_in, 0.0)
    return (renewed, (output, state_in))


def backward_block(grad_state, inputs):
    query_blk, key_blk, value_blk, grad_blk, block_docs, prior_doc, next_doc, state_in = inputs
    doc_mask = same_doc(block_docs)[None]
    scores = jnp.einsum("thd,shd->hts", query_blk, key_blk, preferred_element_type=jnp.float32) / DH
    weights = jnp.where(doc_mask, scores, 0.0).astype(jnp.bfloat16)
    grad_scores = jnp.einsum(
        "the,she->hts", grad_blk, value_blk, preferred_element_type=jnp.float32
    )
    grad_weights = jnp.where(doc_mask, grad_scores, 0.0).astype(jnp.bfloat16)
    grad_query = (
        jnp.einsum("hts,shd->thd", grad_weights, key_blk, preferred_element_type=jnp.float32) / DH
    )
    grad_key = (
        jnp.einsum("hts,thd->shd", grad_weights, query_blk, preferred_element_type=jnp.float32) / DH
    )
    grad_value = jnp.einsum("hts,the->she", weights, grad_blk, preferred_element_type=jnp.float32)
    from_state = (
        jnp.einsum(
            "the,hde->thd",
            grad_blk,
            state_in.astype(jnp.bfloat16),
            preferred_element_type=jnp.float32,
        )
        / DH
    )
    grad_query = grad_query + jnp.where((block_docs == prior_doc)[:, None, None], from_state, 0.0)
    later_mask = (block_docs == next_doc)[:, None, None]
    state_low = grad_state.astype(jnp.bfloat16)
    grad_key = grad_key + jnp.where(
        later_mask,
        jnp.einsum("she,hde->shd", value_blk, state_low, preferred_element_type=jnp.float32) / DH,
        0.0,
    )
    grad_value = grad_value + jnp.where(
        later_mask,
        jnp.einsum("shd,hde->she", key_blk, state_low, preferred_element_type=jnp.float32) / DH,
        0.0,
    )
    head_mask = (block_docs == block_docs[0]).astype(jnp.bfloat16)
    local_sum = jnp.einsum(
        "thd,the->hde",
        query_blk * head_mask[:, None, None],
        grad_blk,
        preferred_element_type=jnp.float32,
    )
    renewed = local_sum + jnp.where(block_docs[0] == next_doc, grad_state, 0.0)
    return (
        renewed,
        (
            grad_query.astype(jnp.bfloat16),
            grad_key.astype(jnp.bfloat16),
            grad_value.astype(jnp.bfloat16),
        ),
    )


def shards(queries, keys, values, d_out, doc_lengths, gain):
    tokens = queries.shape[0]
    width = queries.shape[1]
    heads = width // DH
    blocks = tokens // BLOCK
    position = lax.axis_index(("seq", "rep"))
    first = position * tokens
    doc_ends = jnp.cumsum(doc_lengths)
    places = first + jnp.arange(tokens, dtype=jnp.int32)
    docs = doc_index(doc_ends, places)
    edges = doc_index(doc_ends, jnp.stack([first - 1, first + tokens]))
    before = edges[0]
    after = edges[1]
    flat = (tokens, heads, DH)
    query_all = queries.reshape(flat)
    key_all = keys.reshape(flat)
    value_all = values.reshape(flat)
    tail_mask = (docs == docs[-1]).astype(jnp.bfloat16)
    summary = jnp.einsum(
        "thd,the->hde",
        key_all * tail_mask[:, None, None],
        value_all,
        preferred_element_type=jnp.float32,
    )
    reset = (docs[-1] != before).astype(jnp.float32).reshape(1)
    zero_state = jnp.zeros_like(summary)
    zero_flag = jnp.zeros((1,), jnp.float32)
    state_in = prefix(
        (summary, reset), ("seq", "rep"), carry_state, (zero_state, zero_flag), False
    )[0]
    shaped = (blocks, BLOCK, heads, DH)
    query_blks = queries.reshape(shaped)
    key_blks = keys.reshape(shaped)
    value_blks = values.reshape(shaped)
    doc_blks = docs.reshape(blocks, BLOCK)
    priors = jnp.concatenate([before[None], doc_blks[:-1, -1]])
    nexts = jnp.concatenate([doc_blks[1:, 0], after[None]])
    final_state, (outputs, states) = lax.scan(
        forward_block, state_in, (query_blks, key_blks, value_blks, doc_blks, priors)
    )
    mean_sq = jnp.mean(outputs * outputs, axis=-1, keepdims=True)
    inverse = lax.rsqrt(mean_sq + 1e-05)
    normed = outputs * inverse
    gains = gain.reshape(heads, DH)
    mixed = (normed * gains).astype(jnp.bfloat16)
    grad_out = d_out.reshape(shaped).astype(jnp.float32)
    gain_terms = jnp.sum(grad_out * normed, axis=(0, 1)).reshape(width)
    grad_normed = grad_out * gains
    grad_attn = (
        inverse * (grad_normed - normed * jnp.mean(grad_normed * normed, axis=-1, keepdims=True))
    ).astype(jnp.bfloat16)
    grad_flat = grad_attn.reshape(flat)
    head_mask = (docs == docs[0]).astype(jnp.bfloat16)
    grad_summary = jnp.einsum(
        "thd,the->hde",
        query_all * head_mask[:, None, None],
        grad_flat,
        preferred_element_type=jnp.float32,
    )
    grad_reset = (docs[0] != after).astype(jnp.float32).reshape(1)
    grad_in = prefix(
        (grad_summary, grad_reset), ("seq", "rep"), carry_state, (zero_state, zero_flag), True
    )[0]
    final_grad, (grad_q, grad_k, grad_v) = lax.scan(
        backward_block,
        grad_in,
        (query_blks, key_blks, value_blks, grad_attn, doc_blks, priors, nexts, states),
        reverse=True,
    )
    total_count = lax.axis_size(("seq", "rep")) * tokens
    grad_gain = lax.psum(gain_terms, ("seq", "rep")) / math.sqrt(total_count)
    out_shape = (tokens, width)
    return (
        mixed.reshape(out_shape),
        grad_q.reshape(out_shape),
        grad_k.reshape(out_shape),
        grad_v.reshape(out_shape),
        grad_gain.reshape(1, width),
    )


def solution(mesh):
    return jax.shard_map(
        shards,
        mesh=mesh,
        in_specs=(
            P(("groups", "seq", "rep"), "head"),
            P(("groups", "seq", "rep"), "head"),
            P(("groups", "seq", "rep"), "head"),
            P(("groups", "seq", "rep"), "head"),
            P("groups"),
            P("head"),
        ),
        out_specs=(
            P(("groups", "seq", "rep"), "head"),
            P(("groups", "seq", "rep"), "head"),
            P(("groups", "seq", "rep"), "head"),
            P(("groups", "seq", "rep"), "head"),
            P("groups", "head"),
        ),
        check_vma=False,
    )
```

profile of v0, /device:TPU:0, one launch (start us, length us, event | category | flops | bytes accessed | tf_op | source)
XLA Modules:
  0.0 296.9 jit_solution(5995807785066267221)
XLA Ops:
  9.7 3.5 %copy.85 = bf16[64,8,16,128]{3,2,1,0:T(8,128)(2,1)} copy(bf16[64,8,16,128]{3,1,2,0:T(8,128)(2,1)} %bitcast.117) | data formatting | bytes 4194304
  13.2 4.3 %copy.58 = bf16[512,16,128]{0,2,1:T(8,128)(2,1)} copy(bf16[512,16,128]{2,1,0:T(8,128)(2,1)} %bitcast.122) | data formatting | bytes 4194304 | tf_op jit(solution)/shard_map/while/body/jit(dynamic_index_in_dim)/squeeze | solution.py:161
  20.0 3.3 %fusion.8 = f32[16,128,128]{2,1,0:T(8,128)} fusion(bf16[512,16,128]{0,2,1:T(8,128)(2,1)} %copy.58, bf16[512]{0:T(512)(128)(2,1)S(1)} %get-tuple-element.339, bf16[512,2048]{1,0:T(8,128)(2,1)S(1)} %copy-done), kind=kOutput, calls=%fused_computation.23 | convolution fusion | flops 269484032 | bytes 5243904 | tf_op jit(solution)/shard_map/thd,the->hde/dot_general | solution.py:142
  26.1 18.5 %all-reduce = f32[8]{0:T(128)S(1)} all-reduce(f32[8]{0:T(128)S(1)} %dynamic-update-slice), channel_id=1, replica_groups=mesh['groups'=2,'seq'=4,'head'=2,'rep'=2] {'seq','rep'}, use_global_device_ids=true, to_apply=%add | all-reduce | flops 8 | bytes 64
  44.5 4.0 %copy.82 = bf16[512,2048]{0,1:T(8,128)(2,1)} copy(bf16[512,2048]{1,0:T(8,128)(2,1)} %param.10) | data formatting | bytes 4194304 | tf_op jit(solution)/shard_map/while/body/jit(dynamic_index_in_dim)/squeeze | solution.py:161
  48.5 4.1 %copy.62 = f32[512,2048]{0,1:T(8,128)} copy(bf16[512,2048]{1,0:T(8,128)(2,1)} %param.13) | data formatting | bytes 6291456 | tf_op jit(solution)/shard_map/convert_element_type | solution.py:169
  52.8 8.2 %select_convert_fusion.1 = bf16[16,512,512]{2,1,0:T(8,128)(2,1)} fusion(bf16[512,16,128]{0,2,1:T(8,128)(2,1)} %bitcast.113, pred[512,512]{1,0:T(8,128)(4,1)S(1)} %fusion.23, bf16[512,2048]{1,0:T(8,128)(2,1)} %param.11), kind=kOutput, calls=%fused_computation.7 | convolution fusion | flops 1086324736 | bytes 12845056 | tf_op jit(solution)/shard_map/while/body/eval_jaxpr/thd,shd->hts/dot_general | solution.py:44
  61.1 47.3 %all-gather.5.cloned.1.call-done = f32[128,128,128]{2,1,0:T(8,128)} async-done(((f32[16,128,128]{2,1,0:T(8,128)}), f32[128,128,128]{2,1,0:T(8,128)}) %all-gather.5.cloned.1.call-update) | async-done | bytes 8388624 | tf_op jit(solution)/shard_map/all_gather | solution.py:14
  108.4 23.7 %while.18 = (s32[]{:T(128)}, f32[16,128,128]{2,1,0:T(8,128)S(1)}, s32[]{:T(128)}, f32[8,16,128,128]{3,2,1,0:T(8,128)}, f32[8,1]{0,1:T(1,128)S(1)}, /*index=5*/s32[]{:T(128)}, s32[]{:T(128)}) while((s32[]{:T(128)}, f32[16,128,128]{2,1,0:T(8,128)S(1)}, s32[]{:T(128)}, f32[8,16,128,128]{3,2,1,0:T(8,128)}, f32[8,1]{0,1:T(1,128)S(1)}, ...), condition=%wide.region_4.5_spmd.clone, body=%wide.region_3.4_spmd.clone.sunk | while | flops 1048581 | bytes 3145853 | solution.py:26
  108.9 2.8 fusion.59
  112.3 2.8 fusion.59
  115.7 2.8 fusion.59
  119.1 2.8 fusion.59
  122.5 2.8 fusion.59
  132.1 4.7 %fusion.27 = f32[16,128,512]{2,1,0:T(8,128)} fusion(bf16[512,16,128]{0,2,1:T(8,128)(2,1)} %bitcast.114, f32[16,128,128]{2,1,0:T(8,128)S(1)} %get-tuple-element.259), kind=kOutput, calls=%fused_computation.43 | convolution fusion | flops 268697600 | bytes 7340032 | tf_op jit(solution)/shard_map/while/body/eval_jaxpr/thd,hde->the/dot_general | solution.py:48
  136.7 9.6 %multiply_reduce_fusion.2 = (f32[512,16]{0,1:T(8,128)S(1)}, f32[512,16,128]{0,2,1:T(8,128)}) fusion(f32[16,128,512]{2,1,0:T(8,128)} %fusion.27, pred[512]{0:T(512)(128)(4,1)S(1)} %get-tuple-element.340, bf16[16,512,512]{2,1,0:T(8,128)(2,1)} %select_convert_fusion.1, bf16[512,2048]{1,0:T(8,128)(2,1)S(1)} %copy-done), kind=kOutput, calls=%fused_computation.18 | convolution fusion | flops 1078976512 | bytes 18907648 | tf_op jit(solution)/shard_map/while/body/eval_jaxpr/hts,shd->thd/dot_general | solution.py:46
  146.4 3.5 %multiply_reduce_fusion = (f32[16,128]{1,0:T(8,128)S(1)}, f32[512,16]{0,1:T(8,128)S(1)}) fusion(f32[512,16,128]{0,2,1:T(8,128)S(1)} %bitcast.112, f32[512,16,128]{0,2,1:T(8,128)} %get-tuple-element.347, f32[512,16]{0,1:T(8,128)S(1)} %add_rsqrt_fusion, f32[16,128]{1,0:T(8,128)S(1)} %bitcast.126, f32[512,2048]{0,1:T(8,128)S(1)} %copy-done.1), kind=kLoop, calls=%fused_computation.13 | loop fusion | flops 6281216 | bytes 12664832 | tf_op jit(solution)/shard_map/reduce_sum | solution.py:170
  157.2 15.4 %all-reduce.2 = (f32[8]{0:T(128)S(1)}, f32[2048]{0:T(1024)S(1)}) all-reduce(f32[8]{0:T(128)S(1)} %dynamic-update-slice.1, f32[2048]{0:T(1024)S(1)} %bitcast.125), channel_id=1, replica_groups=mesh['groups'=2,'seq'=4,'head'=2,'rep'=2] {'seq','rep'}, use_global_device_ids=true, to_apply=%add.1 | all-reduce | flops 2056 | bytes 16448
  172.7 3.9 %copy.73 = bf16[512,2048]{1,0:T(8,128)(2,1)} copy(bf16[512,2048]{0,1:T(8,128)(2,1)} %bitcast.123) | data formatting | bytes 4194304
  176.6 4.1 %select_convert_fusion = bf16[16,512,512]{2,1,0:T(8,128)(2,1)S(1)} fusion(bf16[512,16,128]{0,2,1:T(8,128)(2,1)} %copy-done.4, pred[512,512]{1,0:T(8,128)(4,1)S(1)} %fusion.23, bf16[512,2048]{1,0:T(8,128)(2,1)S(1)} %copy-done), kind=kOutput, calls=%fused_computation.6 | convolution fusion | flops 1082130432 | bytes 12845056 | tf_op jit(solution)/shard_map/while/body/eval_jaxpr/the,she->hts/dot_general | solution.py:73
  180.8 8.1 %fusion.34 = f32[16,512,128]{1,2,0:T(8,128)} fusion(bf16[16,512,512]{2,1,0:T(8,128)(2,1)S(1)} %select_convert_fusion, bf16[512,16,128]{0,2,1:T(8,128)(2,1)} %copy.58), kind=kOutput, calls=%fused_computation.61 | convolution fusion | flops 1073741824 | bytes 14680064 | tf_op jit(solution)/shard_map/while/body/eval_jaxpr/hts,shd->thd/dot_general | solution.py:78
  188.8 4.4 %fusion.3 = bf16[512,16,128]{0,2,1:T(8,128)(2,1)} fusion(f32[16,512,128]{1,2,0:T(8,128)} %fusion.34, bf16[512,16,128]{0,2,1:T(8,128)(2,1)S(1)} %copy-done.5, pred[512]{0:T(512)(128)(4,1)S(1)} %get-tuple-element.340, f32[16,128,128]{2,1,0:T(8,128)S(1)} %copy-done.3), kind=kOutput, calls=%fused_computation.11 | convolution fusion | flops 273940480 | bytes 9437696 | tf_op jit(solution)/shard_map/while/body/eval_jaxpr/the,hde->thd/dot_general | solution.py:85
  193.3 3.9 %copy.74 = bf16[512,2048]{1,0:T(8,128)(2,1)} copy(bf16[512,2048]{0,1:T(8,128)(2,1)} %bitcast.119) | data formatting | bytes 4194304
  197.8 7.3 %fusion.35 = f32[16,128,512]{2,1,0:T(8,128)} fusion(bf16[512,16,128]{0,2,1:T(8,128)(2,1)} %copy-done.4, bf16[16,512,512]{2,1,0:T(8,128)(2,1)} %select_convert_fusion.1), kind=kOutput, calls=%fused_computation.62 | convolution fusion | flops 1073741824 | bytes 14680064 | tf_op jit(solution)/shard_map/while/body/eval_jaxpr/hts,the->she/dot_general | solution.py:83
  205.0 31.3 %all-gather.7.cloned.1.call-done = f32[128,128,128]{2,1,0:T(8,128)} async-done(((f32[16,128,128]{2,1,0:T(8,128)}), f32[128,128,128]{2,1,0:T(8,128)}) %all-gather.7.cloned.1.call-update) | async-done | bytes 8388624 | tf_op jit(solution)/shard_map/all_gather | solution.py:14
  236.3 7.7 %rev.6 = f32[8,16,128,128]{3,2,1,0:T(8,128)} reverse(f32[8,16,128,128]{3,2,1,0:T(8,128)} %bitcast.121), dimensions={0} | reverse | bytes 16777216 | tf_op jit(solution)/shard_map/rev | solution.py:16
  244.0 23.7 %while.19 = (s32[]{:T(128)}, f32[16,128,128]{2,1,0:T(8,128)S(1)}, s32[]{:T(128)}, f32[8,16,128,128]{3,2,1,0:T(8,128)}, f32[8,1]{0,1:T(1,128)S(1)}, /*index=5*/s32[]{:T(128)}, s32[]{:T(128)}) while((s32[]{:T(128)}, f32[16,128,128]{2,1,0:T(8,128)S(1)}, s32[]{:T(128)}, f32[8,16,128,128]{3,2,1,0:T(8,128)}, f32[8,1]{0,1:T(1,128)S(1)}, ...), condition=%wide.region_8.9_spmd.clone, body=%wide.region_7.8_spmd.clone.sunk | while | flops 1048581 | bytes 3145853 | solution.py:26
  248.0 2.8 fusion.61
  267.7 2.9 fusion.5
  274.4 3.9 %copy.76 = bf16[512,2048]{1,0:T(8,128)(2,1)} copy(bf16[512,2048]{0,1:T(8,128)(2,1)} %bitcast.120) | data formatting | bytes 4194304
  278.3 7.8 %fusion.2 = bf16[512,16,128]{0,2,1:T(8,128)(2,1)} fusion(f32[16,128,512]{2,1,0:T(8,128)} %fusion.5, bf16[512,16,128]{0,2,1:T(8,128)(2,1)} %bitcast.115, bf16[16,512,512]{2,1,0:T(8,128)(2,1)} %copy-done.7, pred[512]{0:T(512)(128)(4,1)S(1)} %get-tuple-element.338), kind=kOutput, calls=%fused_computation.9 | convolution fusion | flops 1078984704 | bytes 16777728 | tf_op jit(solution)/shard_map/while/body/eval_jaxpr/hts,thd->shd/dot_general | solution.py:81
  286.2 3.9 %copy.75 = bf16[512,2048]{1,0:T(8,128)(2,1)} copy(bf16[512,2048]{0,1:T(8,128)(2,1)} %bitcast.118) | data formatting | bytes 4194304
  (75 shorter events, 47.8 us)
Async XLA Ops:
  7.2 12.8 %copy-start = (bf16[512,2048]{1,0:T(8,128)(2,1)S(1)}, bf16[512,2048]{1,0:T(8,128)(2,1)}, u32[]{:S(2)}) copy-start(bf16[512,2048]{1,0:T(8,128)(2,1)} %param.12) | copy-start | bytes 6291460
  7.2 101.2 %all-gather.5.cloned.1.call-start = ((), (), s32[]{:S(2)}) async-start(), calls=%async_computation | async-start | bytes 9437184 | tf_op jit(solution)/shard_map/all_gather | solution.py:14
  17.5 7.2 %copy-start.12 = (u32[32]{0:T(128)S(1)}, u32[32]{0:T(128)}, u32[]{:S(2)}) copy-start(u32[32]{0:T(128)} %constant.146) | copy-start | bytes 388
  23.3 213.0 %all-gather.7.cloned.1.call-start = ((), (), s32[]{:S(2)}) async-start(), calls=%async_computation.1 | async-start | bytes 9437184 | tf_op jit(solution)/shard_map/all_gather | solution.py:14
  132.1 14.2 %copy-start.2 = (f32[16,128,128]{2,1,0:T(8,128)}, f32[16,128,128]{2,1,0:T(8,128)S(1)}, u32[]{:S(2)}) copy-start(f32[16,128,128]{2,1,0:T(8,128)S(1)} %get-tuple-element.259) | copy-start | bytes 3145732
  136.7 9.6 %copy-start.1 = (f32[512,2048]{0,1:T(8,128)S(1)}, f32[512,2048]{0,1:T(8,128)}, u32[]{:S(2)}) copy-start(f32[512,2048]{0,1:T(8,128)} %copy.62) | copy-start | bytes 12582916
  136.7 9.6 %copy-start.11 = (f32[2048]{0:T(1024)S(1)}, f32[2048]{0:T(1024)}, u32[]{:S(2)}) copy-start(f32[2048]{0:T(1024)} %param.15) | copy-start | bytes 24580
  146.3 3.5 %copy-start.6 = (f32[512,16,128]{0,2,1:T(8,128)S(1)}, f32[512,16,128]{0,2,1:T(8,128)}, u32[]{:S(2)}) copy-start(f32[512,16,128]{0,2,1:T(8,128)} %get-tuple-element.347) | copy-start | bytes 12582916
  149.8 3.7 %copy-start.8 = (bf16[512,2048]{0,1:T(8,128)(2,1)S(1)}, bf16[512,2048]{0,1:T(8,128)(2,1)}, u32[]{:S(2)}) copy-start(bf16[512,2048]{0,1:T(8,128)(2,1)} %copy.82) | copy-start | bytes 6291460
  152.2 1.3 copy-start.4
  180.7 8.1 %copy-start.7 = (bf16[16,512,512]{2,1,0:T(8,128)(2,1)}, bf16[16,512,512]{2,1,0:T(8,128)(2,1)S(1)}, u32[]{:S(2)}) copy-start(bf16[16,512,512]{2,1,0:T(8,128)(2,1)S(1)} %select_convert_fusion) | copy-start | bytes 25165828
  180.7 8.1 %copy-start.3 = (f32[16,128,128]{2,1,0:T(8,128)S(1)}, f32[16,128,128]{2,1,0:T(8,128)}, u32[]{:S(2)}) copy-start(f32[16,128,128]{2,1,0:T(8,128)} %copy-done.2) | copy-start | bytes 3145732
  180.8 8.1 %copy-start.5 = (bf16[512,16,128]{0,2,1:T(8,128)(2,1)S(1)}, bf16[512,16,128]{0,2,1:T(8,128)(2,1)}, u32[]{:S(2)}) copy-start(bf16[512,16,128]{0,2,1:T(8,128)(2,1)} %copy-done.4) | copy-start | bytes 6291460
  267.7 3.4 %copy-start.9 = (f32[16,128,512]{2,1,0:T(8,128)S(1)}, f32[16,128,512]{2,1,0:T(8,128)}, u32[]{:S(2)}) copy-start(f32[16,128,512]{2,1,0:T(8,128)} %fusion.35) | copy-start | bytes 12582916
  267.7 4.4 %copy-start.10 = (bf16[512,2048]{1,0:T(8,128)(2,1)S(1)}, bf16[512,2048]{1,0:T(8,128)(2,1)}, u32[]{:S(2)}) copy-start(bf16[512,2048]{1,0:T(8,128)(2,1)} %param.11) | copy-start | bytes 6291460
Sparse Core Ops, SparseCore 0:
  23.4 84.8 all-gather.4
  155.4 80.8 all-gather.6
where the time goes:
time: 299 us; the launch traced here: 297 us
  waiting for transfers between devices  78.6 us (26%)
  matrix products  64.3 us (22%)
  other arithmetic  57.5 us (19%)
  local copies, waits for them, and re-layouts  45.5 us (15%)
  blocking collectives  33.9 us (11%)
  between operations  16.8 us (6%)
    all_gather x2, waiting for transfers between devices, prefix(): pieces = jax.tree.map(lambda part: lax.all_gather(part, axis), value)  78.6 us
    select_n x14, other arithmetic, hop(): jnp.where(position < mine, new, old)  38.9 us
    unnamed x2, blocking collectives  33.9 us
    unnamed x37, local copies, waits for them, and re-layouts  24.3 us
    dot_general x1, matrix products, forward_block(): jnp.einsum('hts,shd->thd', weights, value_blk, preferred_element_type=jnp...  9.57 us
    dot_general x1, matrix products, forward_block(): jnp.einsum('thd,shd->hts', query_blk, key_blk, preferred_element_type=jnp...  8.23 us
    squeeze x2, local copies, waits for them, and re-layouts, shards(): lax.scan(forward_block, state_in, (query_blks, key_blks, value_blks, doc_...  8.22 us
    sub x14, other arithmetic, carry_state(): 1.0 - latter[1][0]  8.19 us
  transfers between devices with their start and end apart: 2, of which 2 were waited for; matrix products, arithmetic and copies ran while one was open for 17% of the time, Pallas kernels for 0%

commit v1 on v0

v1 whole, which is shorter than its diff:
```python
import functools
import math

import jax
import jax.numpy as jnp
from jax import lax
from jax.experimental import pallas as pl
from jax.experimental.pallas import tpu as pltpu
from jax.sharding import PartitionSpec as P

DH = 128
HALF = 256
MESH = pl.DeviceIdType.MESH
F32 = jnp.float32
BF16 = jnp.bfloat16


def nn(a, b):
    return lax.dot_general(a, b, (((1,), (0,)), ((), ())), preferred_element_type=F32)


def nt(a, b):
    return lax.dot_general(a, b, (((1,), (1,)), ((), ())), preferred_element_type=F32)


def tn(a, b):
    return lax.dot_general(a, b, (((0,), (0,)), ((), ())), preferred_element_type=F32)


def kernel(
    heads, tokens, seqs, reps, ndoc,
    lens, gain, q_hbm, k_hbm, v_hbm, d_hbm,
    mix_hbm, gq_hbm, gk_hbm, gv_hbm, ggain,
    qs, ks, vs, ds, acc, w_top, w_bot, gs, mask, prior_m, next_m, tail_m, head_m,
    fout, fin, bout, bin_, sb, gsb, ob, gslots,
    in_sem, out_sem, fsend, frecv, bsend, brecv, gsend, grecv,
):
    n = seqs * reps
    rank = lax.axis_index("seq") * reps + lax.axis_index("rep")
    total = n * tokens
    first = rank * tokens
    top = slice(0, HALF)
    bot = slice(HALF, 2 * HALF)

    def device(other):
        return {"seq": lax.div(other, reps), "rep": lax.rem(other, reps)}

    def cols(h):
        return pl.ds(pl.multiple_of(h * DH, DH), DH)

    def load(i, hbm, buf, h):
        return pltpu.make_async_copy(hbm.at[:, cols(h)], buf.at[h], in_sem.at[i, h])

    def store(i, hbm, h):
        return pltpu.make_async_copy(ob.at[i, h], hbm.at[:, cols(h)], out_sem.at[i, h])

    def each(fn):
        lax.fori_loop(0, heads, lambda h, c: (fn(h), c)[1], 0)

    def start_kv(h):
        load(0, k_hbm, ks, h).start()
        load(1, v_hbm, vs, h).start()

    def start_qd(h):
        load(2, q_hbm, qs, h).start()
        load(3, d_hbm, ds, h).start()

    each(start_kv)
    each(start_qd)
    barrier = pltpu.get_barrier_semaphore()
    for o in range(1, n):
        pl.semaphore_signal(barrier, inc=1, device_id=device(lax.rem(rank + o, n)), device_id_type=MESH)

    ends = []
    run = jnp.int32(0)
    for i in range(ndoc):
        run = run + lens[i]
        ends.append(run)

    def doc_of(place):
        return sum((jnp.where(e <= place, 1, 0) for e in ends))

    before, after = doc_of(first - 1), doc_of(first + tokens)
    doc_first, doc_last = doc_of(first), doc_of(first + tokens - 1)
    col = lax.broadcasted_iota(jnp.int32, (tokens, DH), 0)
    doc_col = doc_of(col + first)
    prior_m[...] = jnp.where(doc_col == before, 1.0, 0.0)
    next_m[...] = jnp.where(doc_col == after, 1.0, 0.0)
    tail_m[...] = jnp.where(doc_col == doc_last, 1.0, 0.0).astype(BF16)
    head_m[...] = jnp.where(doc_col == doc_first, 1.0, 0.0).astype(BF16)
    place_row = lax.broadcasted_iota(jnp.int32, (8, tokens), 1)
    doc_row = doc_of(place_row + first)
    for j in range(tokens // DH):
        lanes = slice(j * DH, (j + 1) * DH)
        u = place_row[0:1, lanes]
        keep = (doc_col == doc_row[0:1, lanes]) & (col >= u)
        mask[:, lanes] = jnp.where(keep, 1.0 / DH, 0.0)
    pass_f = jnp.where(doc_last == before, 1.0, 0.0)
    pass_b = jnp.where(doc_first == after, 1.0, 0.0)

    @pl.when(rank == 0)
    def _():
        fin[...] = jnp.zeros_like(fin)

    @pl.when(rank == n - 1)
    def _():
        bin_[...] = jnp.zeros_like(bin_)

    def local(h):
        load(0, k_hbm, ks, h).wait()
        load(1, v_hbm, vs, h).wait()
        fout[h] = tn(ks[h] * tail_m[...], vs[h])

    each(local)
    pl.semaphore_wait(barrier, n - 1)

    def fcopy(h):
        return pltpu.make_async_remote_copy(
            src_ref=fout.at[h], dst_ref=fin.at[h], send_sem=fsend.at[h], recv_sem=frecv.at[h],
            device_id=device(jnp.minimum(rank + 1, n - 1)), device_id_type=MESH,
        )

    def bcopy(h):
        return pltpu.make_async_remote_copy(
            src_ref=bout.at[h], dst_ref=bin_.at[h], send_sem=bsend.at[h], recv_sem=brecv.at[h],
            device_id=device(jnp.maximum(rank - 1, 0)), device_id_type=MESH,
        )

    def gcopy(o):
        return pltpu.make_async_remote_copy(
            src_ref=gslots.at[rank], dst_ref=gslots.at[rank], send_sem=gsend.at[o], recv_sem=grecv.at[rank],
            device_id=device(lax.rem(rank + o, n)), device_id_type=MESH,
        )

    def scores(h):
        load(2, q_hbm, qs, h).wait()
        w_top[h] = (nt(qs[h, top], ks[h, top]) * mask[top, top]).astype(BF16)
        w_bot[h] = (nt(qs[h, bot], ks[h]) * mask[bot]).astype(BF16)
        acc[h, top] = nn(w_top[h], vs[h, top])
        acc[h, bot] = nn(w_bot[h], vs[h])

    def forward(h):
        @pl.when(rank > 0)
        def _():
            fcopy(h).wait_recv()

        fout[h] = fout[h] + pass_f * fin[h]

        @pl.when(rank < n - 1)
        def _():
            fcopy(h).start()

        load(3, d_hbm, ds, h).wait()
        sb[h] = (fin[h] * (1.0 / DH)).astype(BF16)
        attn = acc[h] + prior_m[...] * nn(qs[h], sb[h])
        inverse = lax.rsqrt(jnp.mean(attn * attn, axis=-1, keepdims=True) + 1e-5)
        normed = attn * inverse
        gains = gain[pl.ds(h, 1), :]
        ob[0, h] = (normed * gains).astype(BF16)
        store(0, mix_hbm, h).start()
        d = ds[h].astype(F32)
        terms = d * normed
        gslots[rank, pl.ds(h, 1), :] = jnp.sum(terms, axis=0, keepdims=True)
        g = d * gains
        inner = jnp.mean(g * normed, axis=-1, keepdims=True)
        grad = (inverse * (g - normed * inner)).astype(BF16)
        gs[h] = grad
        bout[h] = tn(qs[h] * head_m[...], grad)

    def backward(h):
        @pl.when(rank < n - 1)
        def _():
            bcopy(h).wait_recv()

        bout[h] = bout[h] + pass_b * bin_[h]

        @pl.when(rank > 0)
        def _():
            bcopy(h).start()

        gsb[h] = (bin_[h] * (1.0 / DH)).astype(BF16)

    def grads(h):
        gt = (nt(gs[h, top], vs[h, top]) * mask[top, top]).astype(BF16)
        gb = (nt(gs[h, bot], vs[h]) * mask[bot]).astype(BF16)
        from_state = prior_m[...] * nt(gs[h], sb[h])
        ob[1, h, top] = (nn(gt, ks[h, top]) + from_state[top]).astype(BF16)
        ob[1, h, bot] = (nn(gb, ks[h]) + from_state[bot]).astype(BF16)
        store(1, gq_hbm, h).start()
        later = next_m[...] * nt(vs[h], gsb[h])
        low = tn(gb, qs[h, bot])
        ob[2, h, top] = (tn(gt, qs[h, top]) + low[top] + later[top]).astype(BF16)
        ob[2, h, bot] = (low[bot] + later[bot]).astype(BF16)
        store(2, gk_hbm, h).start()
        later = next_m[...] * nn(ks[h], gsb[h])
        low = tn(w_bot[h], gs[h, bot])
        ob[3, h, top] = (tn(w_top[h], gs[h, top]) + low[top] + later[top]).astype(BF16)
        ob[3, h, bot] = (low[bot] + later[bot]).astype(BF16)
        store(3, gv_hbm, h).start()

    d1 = lax.div(rank * heads, n - 1)
    d3 = d1 + 1 + lax.div((n - 1 - rank) * heads, n - 1)
    d4 = d3 + 1

    def stage(i, delay, fn):
        @pl.when((i >= delay) & (i < delay + heads))
        def _():
            fn(i - delay)

    def step(i, c):
        stage(i, 0, scores)
        stage(i, d1, forward)

        @pl.when(i == d1 + heads - 1)
        def _():
            for o in range(1, n):
                gcopy(o).start()

        stage(i, d3, backward)
        stage(i, d4, grads)
        return c

    lax.fori_loop(0, d4 + heads, step, 0)

    for o in range(1, n):
        src = lax.rem(rank + n - o, n)
        pltpu.make_async_remote_copy(
            src_ref=gslots.at[src], dst_ref=gslots.at[src], send_sem=gsend.at[o], recv_sem=grecv.at[src],
            device_id=device(src), device_id_type=MESH,
        ).wait_recv()
        gcopy(o).wait_send()
    summed = gslots[0]
    for i in range(1, n):
        summed = summed + gslots[i]
    ggain[...] = summed * (1.0 / math.sqrt(total))

    def finish(h):
        @pl.when(rank < n - 1)
        def _():
            fcopy(h).wait_send()

        @pl.when(rank > 0)
        def _():
            bcopy(h).wait_send()

        store(0, mix_hbm, h).wait()
        store(1, gq_hbm, h).wait()
        store(2, gk_hbm, h).wait()
        store(3, gv_hbm, h).wait()

    each(finish)


def shards(queries, keys, values, d_out, doc_lengths, gain):
    tokens, width = queries.shape
    heads = width // DH
    seqs, reps = lax.axis_size("seq"), lax.axis_size("rep")
    n = seqs * reps
    slab = pltpu.VMEM((heads, tokens, DH), BF16)
    state = pltpu.VMEM((heads, DH, DH), F32)
    state_low = pltpu.VMEM((heads, DH, DH), BF16)
    dma = pltpu.SemaphoreType.DMA
    big = jax.ShapeDtypeStruct((tokens, width), BF16)
    hbm = pl.BlockSpec(memory_space=pl.ANY)
    vmem = pl.BlockSpec(memory_space=pltpu.VMEM)
    out = pl.pallas_call(
        functools.partial(kernel, heads, tokens, seqs, reps, doc_lengths.shape[0]),
        out_shape=(big, big, big, big, jax.ShapeDtypeStruct((heads, DH), F32)),
        in_specs=[pl.BlockSpec(memory_space=pltpu.SMEM), vmem, hbm, hbm, hbm, hbm],
        out_specs=(hbm, hbm, hbm, hbm, vmem),
        scratch_shapes=[
            slab, slab, slab, slab,
            pltpu.VMEM((heads, tokens, DH), F32),
            pltpu.VMEM((heads, HALF, HALF), BF16),
            pltpu.VMEM((heads, HALF, 2 * HALF), BF16),
            slab,
            pltpu.VMEM((tokens, tokens), F32),
            pltpu.VMEM((tokens, DH), F32),
            pltpu.VMEM((tokens, DH), F32),
            pltpu.VMEM((tokens, DH), BF16),
            pltpu.VMEM((tokens, DH), BF16),
            state, state, state, state, state_low, state_low,
            pltpu.VMEM((4, heads, tokens, DH), BF16),
            pltpu.VMEM((n, heads, DH), F32),
            dma((4, heads)), dma((4, heads)),
            dma((heads,)), dma((heads,)), dma((heads,)), dma((heads,)),
            dma((n,)), dma((n,)),
        ],
        compiler_params=pltpu.CompilerParams(
            collective_id=0, has_side_effects=True, vmem_limit_bytes=52 << 20
        ),
    )(doc_lengths, gain.reshape(heads, DH), queries, keys, values, d_out)
    return (*out[:4], out[4].reshape(1, width))


def solution(mesh):
    token = P(("groups", "seq", "rep"), "head")
    return jax.shard_map(
        shards,
        mesh=mesh,
        in_specs=(token, token, token, token, P("groups"), P("head")),
        out_specs=(token, token, token, token, P("groups", "head")),
        check_vma=False,
    )
```

time: 299 us -> 80.5 us (0.27)
  waiting for transfers between devices: 78.6 us -> 0 us
  Pallas kernels: 0 us -> 68.4 us
  matrix products: 64.3 us -> 0 us
  other arithmetic: 57.5 us -> 0 us
  local copies, waits for them, and re-layouts: 45.5 us -> 11.3 us
  blocking collectives: 33.9 us -> 0 us
  between operations: 16.8 us -> 0.66 us
    all_gather x2 -> x0, waiting for transfers between devices: 78.6 us -> none  [prefix(): pieces = jax.tree.map(lambda part: lax.all_gather(part, axis), value)]
    pallas_call x0 -> x1, Pallas kernels: none -> 68.4 us  [shards(): pl.pallas_call(functools.partial(kernel, heads, tokens, seqs, reps, doc_l...]
    dot_general x12 -> x0, matrix products: 64.3 us -> none  [the longest x1 9.57 us: forward_block(): jnp.einsum('hts,shd->thd', weights, value_blk, preferred_element_type=jnp...]
    select_n x14 -> x0, other arithmetic: 38.9 us -> none  [hop(): jnp.where(position < mine, new, old)]
    unnamed x2 -> x0, blocking collectives: 33.9 us -> none
    unnamed x37 -> x15, local copies, waits for them, and re-layouts: 24.3 us -> 11.3 us
    squeeze x2 -> x0, local copies, waits for them, and re-layouts: 8.22 us -> none  [shards(): lax.scan(forward_block, state_in, (query_blks, key_blks, value_blks, doc_...]
    sub x14 -> x0, other arithmetic: 8.19 us -> none  [carry_state(): 1.0 - latter[1][0]]
  transfers between devices with their start and end apart: 2 -> 0, of which waited for: 2 -> 0; matrix products, arithmetic and copies ran while one was open for 17% -> 0% of each run, Pallas kernels for 0% -> 0%
where the time goes in v1:
time: 80.5 us; the launch traced here: 80.3 us
  Pallas kernels  68.4 us (85%)
  local copies, waits for them, and re-layouts  11.3 us (14%)
    pallas_call x1, Pallas kernels, shards(): pl.pallas_call(functools.partial(kernel, heads, tokens, seqs, reps, doc_l...  68.4 us
    unnamed x15, local copies, waits for them, and re-layouts  11.3 us

profile of v1, /device:TPU:0, one launch (start us, length us, event | category | flops | bytes accessed | tf_op | source)
XLA Modules:
  0.0 80.3 jit_solution(14071776421265206050)
XLA Ops:
  0.6 0.0 copy-start
  0.6 0.7 copy-done
  1.3 0.0 copy-start.1
  1.3 0.7 copy-done.1
  2.0 68.4 %shard_map.101 = (bf16[512,2048]{1,0:T(8,128)(2,1)}, bf16[512,2048]{1,0:T(8,128)(2,1)}, bf16[512,2048]{1,0:T(8,128)(2,1)}, bf16[512,2048]{1,0:T(8,128)(2,1)}, f32[16,128]{1,0:T(8,128)S(1)}) custom-call(s32[8]{0:T(128)S(1)} %copy-done.1, f32[16,128]{1,0:T(8,128)S(1)} %bitcast.2, bf16[512,2048]{1,0:T(8,128)(2,1)} %q_hbm.1, bf16[512,2048]{1,0:T(8,128)(2,1)} %k_hbm.1, ...), custom_call_target="tpu_custom_call" | custom-call | tf_op jit(solution)/shard_map/pallas_call | solution.py:266
  70.4 0.0 copy-start.4
  70.4 3.3 %copy.16 = bf16[512,2048]{1,0:T(8,128)(2,1)} copy(bf16[512,2048]{1,0:T(8,128)(2,1)} %get-tuple-element.20) | data formatting | bytes 4194304
  73.7 0.0 copy-done.4
  73.7 0.0 copy-start.3
  73.7 1.3 %copy.17 = bf16[512,2048]{1,0:T(8,128)(2,1)} copy(bf16[512,2048]{1,0:T(8,128)(2,1)S(1)} %copy-done.4) | data formatting | bytes 4194304
  75.0 1.0 %copy-done.3 = bf16[512,2048]{1,0:T(8,128)(2,1)S(1)} copy-done((bf16[512,2048]{1,0:T(8,128)(2,1)S(1)}, bf16[512,2048]{1,0:T(8,128)(2,1)}, u32[]{:S(2)}) %copy-start.3) | copy-done | bytes 2097176
  76.0 0.0 copy-start.2
  76.0 1.3 %copy.18 = bf16[512,2048]{1,0:T(8,128)(2,1)} copy(bf16[512,2048]{1,0:T(8,128)(2,1)S(1)} %copy-done.3) | data formatting | bytes 4194304
  77.4 1.0 %copy-done.2 = bf16[512,2048]{1,0:T(8,128)(2,1)S(1)} copy-done((bf16[512,2048]{1,0:T(8,128)(2,1)S(1)}, bf16[512,2048]{1,0:T(8,128)(2,1)}, u32[]{:S(2)}) %copy-start.2) | copy-done | bytes 2097176
  78.4 1.3 %copy.19 = bf16[512,2048]{1,0:T(8,128)(2,1)} copy(bf16[512,2048]{1,0:T(8,128)(2,1)S(1)} %copy-done.2) | data formatting | bytes 4194304
  79.7 0.6 copy.20
Async XLA Ops:
  0.6 0.7 copy-start
  1.3 0.7 copy-start.1
  70.4 3.3 %copy-start.4 = (bf16[512,2048]{1,0:T(8,128)(2,1)S(1)}, bf16[512,2048]{1,0:T(8,128)(2,1)}, u32[]{:S(2)}) copy-start(bf16[512,2048]{1,0:T(8,128)(2,1)} %get-tuple-element.21) | copy-start | bytes 6291460
  73.7 2.3 %copy-start.3 = (bf16[512,2048]{1,0:T(8,128)(2,1)S(1)}, bf16[512,2048]{1,0:T(8,128)(2,1)}, u32[]{:S(2)}) copy-start(bf16[512,2048]{1,0:T(8,128)(2,1)} %get-tuple-element.22) | copy-start | bytes 6291460
  76.0 2.3 %copy-start.2 = (bf16[512,2048]{1,0:T(8,128)(2,1)S(1)}, bf16[512,2048]{1,0:T(8,128)(2,1)}, u32[]{:S(2)}) copy-start(bf16[512,2048]{1,0:T(8,128)(2,1)} %get-tuple-element.23) | copy-start | bytes 6291460

commit v2 on v1

v2 whole, which is shorter than its diff:
```python
import functools
import math

import jax
import jax.numpy as jnp
from jax import lax
from jax.experimental import pallas as pl
from jax.experimental.pallas import tpu as pltpu
from jax.sharding import PartitionSpec as P

DH = 128
HALF = 256
F_BASE, F_HOP, G_LAG, G_HOP = 9, 5, 2, 5
MESH = pl.DeviceIdType.MESH
F32 = jnp.float32
BF16 = jnp.bfloat16


def nn(a, b):
    return lax.dot_general(a, b, (((1,), (0,)), ((), ())), preferred_element_type=F32)


def nt(a, b):
    return lax.dot_general(a, b, (((1,), (1,)), ((), ())), preferred_element_type=F32)


def tn(a, b):
    return lax.dot_general(a, b, (((0,), (0,)), ((), ())), preferred_element_type=F32)


def kernel(
    heads, tokens, seqs, reps, ndoc,
    lens_hbm, gain_hbm, q_hbm, k_hbm, v_hbm, d_hbm,
    mix, gq, gk, gv, ggain,
    lens, gain, qs, ks, vs, ds, acc, w_top, w_bot, gs, mask, prior_m, next_m, tail_m, head_m,
    fown, fpart, fin, fout, frel, fstate,
    bown, bpart, bin_, bout, brel, bstate,
    sb, gsb, gslots,
    in_sem, small_sem, fsem, bsem, gsend, grecv,
):
    n = seqs * reps
    chip, core = lax.axis_index("seq"), lax.axis_index("rep")
    rank = chip * reps + core
    total = n * tokens
    first = rank * tokens
    top = slice(0, HALF)
    bot = slice(HALF, 2 * HALF)

    def device(other):
        return {"seq": lax.div(other, reps), "rep": lax.rem(other, reps)}

    def cols(h):
        return pl.ds(pl.multiple_of(h * DH, DH), DH)

    def load(i, hbm, buf, h):
        return pltpu.make_async_copy(hbm.at[:, cols(h)], buf.at[h], in_sem.at[i, h])

    def each(fn):
        lax.fori_loop(0, heads, lambda h, c: (fn(h), c)[1], 0)

    def start_kv(h):
        load(0, k_hbm, ks, h).start()
        load(1, v_hbm, vs, h).start()

    def start_qd(h):
        load(2, q_hbm, qs, h).start()
        load(3, d_hbm, ds, h).start()

    lens_copy = pltpu.make_async_copy(lens_hbm, lens, small_sem.at[0])
    gain_copy = pltpu.make_async_copy(gain_hbm, gain, small_sem.at[1])
    lens_copy.start()
    gain_copy.start()
    each(start_kv)
    each(start_qd)
    barrier = pltpu.get_barrier_semaphore()
    for o in range(1, n):
        pl.semaphore_signal(barrier, inc=1, device_id=device(lax.rem(rank + o, n)), device_id_type=MESH)

    lens_copy.wait()
    gain_copy.wait()

    ends = []
    run = jnp.int32(0)
    for i in range(ndoc):
        run = run + lens[i]
        ends.append(run)

    def doc_of(place):
        return sum((jnp.where(e <= place, 1, 0) for e in ends))

    before, after = doc_of(first - 1), doc_of(first + tokens)
    doc_first, doc_last = doc_of(first), doc_of(first + tokens - 1)
    col = lax.broadcasted_iota(jnp.int32, (tokens, DH), 0)
    doc_col = doc_of(col + first)
    prior_m[...] = jnp.where(doc_col == before, 1.0, 0.0)
    next_m[...] = jnp.where(doc_col == after, 1.0, 0.0)
    tail_m[...] = jnp.where(doc_col == doc_last, 1.0, 0.0).astype(BF16)
    head_m[...] = jnp.where(doc_col == doc_first, 1.0, 0.0).astype(BF16)
    place_row = lax.broadcasted_iota(jnp.int32, (8, tokens), 1)
    doc_row = doc_of(place_row + first)
    for j in range(tokens // DH):
        lanes = slice(j * DH, (j + 1) * DH)
        u = place_row[0:1, lanes]
        keep = (doc_col == doc_row[0:1, lanes]) & (col >= u)
        mask[:, lanes] = jnp.where(keep, 1.0 / DH, 0.0)

    def carries(one, other):
        return jnp.where(doc_of(one) == doc_of(other), 1.0, 0.0)

    base = chip * reps * tokens
    flags_f = [carries(base + i * tokens - 1, base + (i + 1) * tokens - 1) for i in range(2)]
    flags_b = [carries(base + i * tokens, base + (i + 1) * tokens) for i in (1, 0)]

    @pl.when(chip == 0)
    def _():
        fin[...] = jnp.zeros_like(fin)

    @pl.when(chip == seqs - 1)
    def _():
        bin_[...] = jnp.zeros_like(bin_)

    other_core = {"rep": 1 - core}

    def remote(src, dst, sems, kind, p, where):
        return pltpu.make_async_remote_copy(
            src_ref=src.at[p] if kind else src, dst_ref=dst.at[p],
            send_sem=sems.at[kind, 0, p], recv_sem=sems.at[kind, 1, p],
            device_id=where, device_id_type=MESH,
        )

    class Chain:
        def __init__(self, own, part, arrived, out, rel, state, sems, low, late, flags, ends, onward):
            self.own, self.part, self.arrived, self.out = own, part, arrived, out
            self.rel, self.state, self.sems, self.low = rel, state, sems, low
            f0, f1 = flags
            self.c_own, self.c_part = jnp.where(late, 1.0, f1), jnp.where(late, f1, 1.0)
            self.c_in = f0 * f1
            self.own_part, self.own_in = jnp.where(late, 1.0, 0.0), jnp.where(late, f0, 1.0)
            self.rel_own, self.rel_in = jnp.where(late, 0.0, 1.0), jnp.where(late, 1.0, f0)
            self.is_first, self.is_last = ends
            self.onward = onward

        def to_partner(self, h):
            p = lax.div(h, 2)
            return remote(self.own.at[h], self.part, self.sems, 0, p, other_core)

        def to_next(self, p):
            return remote(self.out, self.arrived, self.sems, 1, p, self.onward)

        def relay(self, p):
            return remote(self.rel, self.state, self.sems, 2, p, other_core)

        def send_own(self, h):
            @pl.when(lax.rem(h, 2) != core)
            def _():
                self.to_partner(h).start()

        def step(self, h):
            @pl.when(lax.rem(h, 2) == core)
            def _():
                p = lax.div(h, 2)
                self.to_partner(h).wait_recv()

                @pl.when(jnp.logical_not(self.is_first))
                def _():
                    self.to_next(p).wait_recv()

                own, part, came = self.own[h], self.part[p], self.arrived[p]

                @pl.when(jnp.logical_not(self.is_last))
                def _():
                    self.out[p] = self.c_own * own + self.c_part * part + self.c_in * came
                    self.to_next(p).start()

                self.rel[p] = self.rel_own * own + self.rel_in * came
                self.relay(p).start()
                self.low[h] = ((self.own_part * part + self.own_in * came) * (1.0 / DH)).astype(BF16)

        def take(self, h):
            @pl.when(lax.rem(h, 2) != core)
            def _():
                p = lax.div(h, 2)
                self.relay(p).wait_recv()
                self.low[h] = (self.state[p] * (1.0 / DH)).astype(BF16)

        def finish(self, h):
            p = lax.div(h, 2)

            @pl.when(lax.rem(h, 2) != core)
            def _():
                self.to_partner(h).wait_send()

            @pl.when(lax.rem(h, 2) == core)
            def _():
                self.relay(p).wait_send()

                @pl.when(jnp.logical_not(self.is_last))
                def _():
                    self.to_next(p).wait_send()

    ahead = Chain(
        fown, fpart, fin, fout, frel, fstate, fsem, sb, core == 1, flags_f,
        (chip == 0, chip == seqs - 1), {"seq": jnp.minimum(chip + 1, seqs - 1)},
    )
    back = Chain(
        bown, bpart, bin_, bout, brel, bstate, bsem, gsb, core == 0, flags_b,
        (chip == seqs - 1, chip == 0), {"seq": jnp.maximum(chip - 1, 0)},
    )

    pl.semaphore_wait(barrier, n - 1)

    def local(h):
        load(0, k_hbm, ks, h).wait()
        load(1, v_hbm, vs, h).wait()
        fown[h] = tn(ks[h] * tail_m[...], vs[h])
        ahead.send_own(h)

    def gcopy(o):
        return pltpu.make_async_remote_copy(
            src_ref=gslots.at[rank], dst_ref=gslots.at[rank], send_sem=gsend.at[o], recv_sem=grecv.at[rank],
            device_id=device(lax.rem(rank + o, n)), device_id_type=MESH,
        )

    def scores(h):
        load(2, q_hbm, qs, h).wait()
        w_top[h] = (nt(qs[h, top], ks[h, top]) * mask[top, top]).astype(BF16)
        w_bot[h] = (nt(qs[h, bot], ks[h]) * mask[bot]).astype(BF16)
        acc[h, top] = nn(w_top[h], vs[h, top])
        acc[h, bot] = nn(w_bot[h], vs[h])

    def forward(h):
        ahead.take(h)
        load(3, d_hbm, ds, h).wait()
        attn = acc[h] + prior_m[...] * nn(qs[h], sb[h])
        inverse = lax.rsqrt(jnp.mean(attn * attn, axis=-1, keepdims=True) + 1e-5)
        normed = attn * inverse
        gains = gain[pl.ds(h, 1), :]
        mix[:, cols(h)] = (normed * gains).astype(BF16)
        d = ds[h].astype(F32)
        terms = d * normed
        gslots[rank, pl.ds(h, 1), :] = jnp.sum(terms, axis=0, keepdims=True)
        g = d * gains
        inner = jnp.mean(g * normed, axis=-1, keepdims=True)
        grad = (inverse * (g - normed * inner)).astype(BF16)
        gs[h] = grad
        bown[h] = tn(qs[h] * head_m[...], grad)
        back.send_own(h)

    def grads(h):
        back.take(h)
        gt = (nt(gs[h, top], vs[h, top]) * mask[top, top]).astype(BF16)
        gb = (nt(gs[h, bot], vs[h]) * mask[bot]).astype(BF16)
        from_state = prior_m[...] * nt(gs[h], sb[h])
        gq[top, cols(h)] = (nn(gt, ks[h, top]) + from_state[top]).astype(BF16)
        gq[bot, cols(h)] = (nn(gb, ks[h]) + from_state[bot]).astype(BF16)
        later = next_m[...] * nt(vs[h], gsb[h])
        low = tn(gb, qs[h, bot])
        gk[top, cols(h)] = (tn(gt, qs[h, top]) + low[top] + later[top]).astype(BF16)
        gk[bot, cols(h)] = (low[bot] + later[bot]).astype(BF16)
        later = next_m[...] * nn(ks[h], gsb[h])
        low = tn(w_bot[h], gs[h, bot])
        gv[top, cols(h)] = (tn(w_top[h], gs[h, top]) + low[top] + later[top]).astype(BF16)
        gv[bot, cols(h)] = (low[bot] + later[bot]).astype(BF16)

    def ahead_done(i):
        due = F_BASE + F_HOP * chip
        spread = jnp.where(chip == 0, i - 2, lax.div(jnp.maximum(i - due + 1, 0) * 5, 9))
        spread = jnp.minimum(spread, i)
        return jnp.clip(jnp.maximum(spread, i - 2 * heads + 1), 0, heads)

    def back_done(i):
        due = 2 * heads + G_LAG + G_HOP * (seqs - 1 - chip)
        return jnp.clip(i + 1 - jnp.minimum(due, 3 * heads), 0, heads)

    def stage(i, delay, fn):
        @pl.when((i >= delay) & (i < delay + heads))
        def _():
            fn(i - delay)

    def chain_steps(chain, low, high):
        lax.fori_loop(low, high, lambda h, c: (chain.step(h), c)[1], 0)

    def step(i, c):
        stage(i, 0, local)
        stage(i, heads, scores)
        chain_steps(ahead, ahead_done(i - 1), ahead_done(i))
        stage(i, 2 * heads, forward)

        @pl.when(i == 3 * heads - 1)
        def _():
            for o in range(1, n):
                gcopy(o).start()

        chain_steps(back, back_done(i - 1), back_done(i))
        stage(i, 3 * heads, grads)
        return c

    lax.fori_loop(0, 4 * heads, step, 0)

    for o in range(1, n):
        src = lax.rem(rank + n - o, n)
        pltpu.make_async_remote_copy(
            src_ref=gslots.at[src], dst_ref=gslots.at[src], send_sem=gsend.at[o], recv_sem=grecv.at[src],
            device_id=device(src), device_id_type=MESH,
        ).wait_recv()
        gcopy(o).wait_send()
    summed = gslots[0]
    for i in range(1, n):
        summed = summed + gslots[i]
    ggain[...] = summed * (1.0 / math.sqrt(total))

    def finish(h):
        ahead.finish(h)
        back.finish(h)

    each(finish)


def shards(queries, keys, values, d_out, doc_lengths, gain):
    tokens, width = queries.shape
    heads = width // DH
    seqs, reps = lax.axis_size("seq"), lax.axis_size("rep")
    n = seqs * reps
    slab = pltpu.VMEM((heads, tokens, DH), BF16)
    state = pltpu.VMEM((heads, DH, DH), F32)
    state_low = pltpu.VMEM((heads, DH, DH), BF16)
    half = pltpu.VMEM((heads // 2, DH, DH), F32)
    dma = pltpu.SemaphoreType.DMA
    big = jax.ShapeDtypeStruct((tokens, width), BF16)
    hbm = pl.BlockSpec(memory_space=pltpu.HBM)
    vmem = pl.BlockSpec(memory_space=pltpu.VMEM)
    out = pl.pallas_call(
        functools.partial(kernel, heads, tokens, seqs, reps, doc_lengths.shape[0]),
        out_shape=(big, big, big, big, jax.ShapeDtypeStruct((heads, DH), F32)),
        in_specs=[hbm] * 6,
        out_specs=(vmem,) * 5,
        scratch_shapes=[
            pltpu.SMEM(doc_lengths.shape, jnp.int32),
            pltpu.VMEM((heads, DH), F32),
            slab, slab, slab, slab,
            pltpu.VMEM((heads, tokens, DH), F32),
            pltpu.VMEM((heads, HALF, HALF), BF16),
            pltpu.VMEM((heads, HALF, 2 * HALF), BF16),
            slab,
            pltpu.VMEM((tokens, tokens), F32),
            pltpu.VMEM((tokens, DH), F32),
            pltpu.VMEM((tokens, DH), F32),
            pltpu.VMEM((tokens, DH), BF16),
            pltpu.VMEM((tokens, DH), BF16),
            state, half, half, half, half, half,
            state, half, half, half, half, half,
            state_low, state_low,
            pltpu.VMEM((n, heads, DH), F32),
            dma((4, heads)), dma((2,)), dma((3, 2, heads // 2)), dma((3, 2, heads // 2)),
            dma((n,)), dma((n,)),
        ],
        compiler_params=pltpu.CompilerParams(
            collective_id=0, has_side_effects=True, vmem_limit_bytes=44 << 20
        ),
    )(doc_lengths, gain.reshape(heads, DH), queries, keys, values, d_out)
    return (*out[:4], out[4].reshape(1, width))


def solution(mesh):
    token = P(("groups", "seq", "rep"), "head")
    return jax.shard_map(
        shards,
        mesh=mesh,
        in_specs=(token, token, token, token, P("groups"), P("head")),
        out_specs=(token, token, token, token, P("groups", "head")),
        check_vma=False,
    )
```

time: 80.5 us -> 73.5 us (0.913)
  local copies, waits for them, and re-layouts: 11.3 us -> 7.22 us
  Pallas kernels: 68.4 us -> 65.5 us
    unnamed x15 -> x9, local copies, waits for them, and re-layouts: 11.3 us -> 7.22 us
    pallas_call x1, Pallas kernels: 68.4 us -> 65.5 us  [shards(): pl.pallas_call(functools.partial(kernel, heads, tokens, seqs, reps, doc_l...]
where the time goes in v2:
time: 73.5 us; the launch traced here: 73.3 us
  Pallas kernels  65.5 us (89%)
  local copies, waits for them, and re-layouts  7.22 us (10%)
    pallas_call x1, Pallas kernels, shards(): pl.pallas_call(functools.partial(kernel, heads, tokens, seqs, reps, doc_l...  65.5 us
    unnamed x9, local copies, waits for them, and re-layouts  7.22 us

profile of v2, /device:TPU:0, one launch (start us, length us, event | category | flops | bytes accessed | tf_op | source)
XLA Modules:
  0.0 73.3 jit_solution(11932857794845397671)
XLA Ops:
  0.6 0.0 copy-start
  0.6 0.7 copy-done
  1.3 0.0 copy-start.1
  1.3 0.7 copy-done.1
  2.0 65.5 %shard_map.101 = (bf16[512,2048]{1,0:T(8,128)(2,1)S(1)}, bf16[512,2048]{1,0:T(8,128)(2,1)S(1)}, bf16[512,2048]{1,0:T(8,128)(2,1)S(1)}, bf16[512,2048]{1,0:T(8,128)(2,1)S(1)}, f32[16,128]{1,0:T(8,128)S(1)}) custom-call(s32[8]{0:T(128)S(1)} %copy-done.1, f32[16,128]{1,0:T(8,128)S(1)} %bitcast.2, bf16[512,2048]{1,0:T(8,128)(2,1)} %q_hbm.1, ...), custom_call_target="tpu_custom_call" | custom-call | tf_op jit(solution)/shard_map/pallas_call | solution.py:332
  67.5 1.3 %copy.16 = bf16[512,2048]{1,0:T(8,128)(2,1)} copy(bf16[512,2048]{1,0:T(8,128)(2,1)S(1)} %get-tuple-element.20) | data formatting | bytes 4194304
  68.8 1.3 %copy.17 = bf16[512,2048]{1,0:T(8,128)(2,1)} copy(bf16[512,2048]{1,0:T(8,128)(2,1)S(1)} %get-tuple-element.21) | data formatting | bytes 4194304
  70.1 1.3 %copy.18 = bf16[512,2048]{1,0:T(8,128)(2,1)} copy(bf16[512,2048]{1,0:T(8,128)(2,1)S(1)} %get-tuple-element.22) | data formatting | bytes 4194304
  71.4 1.3 %copy.19 = bf16[512,2048]{1,0:T(8,128)(2,1)} copy(bf16[512,2048]{1,0:T(8,128)(2,1)S(1)} %get-tuple-element.23) | data formatting | bytes 4194304
  72.7 0.6 copy.20
Async XLA Ops:
  0.6 0.7 copy-start
  1.3 0.7 copy-start.1

commit v3 on v2

--- a/solution.py
+++ b/solution.py
@@ -10,7 +10,7 @@
 
 DH = 128
 HALF = 256
-F_BASE, F_HOP, G_LAG, G_HOP = 9, 5, 2, 5
+F_BASE, F_HOP, G_LAG, G_HOP = 4, 4, 1, 3
 MESH = pl.DeviceIdType.MESH
 F32 = jnp.float32
 BF16 = jnp.bfloat16
@@ -167,13 +167,13 @@
 
                 own, part, came = self.own[h], self.part[p], self.arrived[p]
 
+                self.rel[p] = self.rel_own * own + self.rel_in * came
+                self.relay(p).start()
                 @pl.when(jnp.logical_not(self.is_last))
                 def _():
                     self.out[p] = self.c_own * own + self.c_part * part + self.c_in * came
                     self.to_next(p).start()
 
-                self.rel[p] = self.rel_own * own + self.rel_in * came
-                self.relay(p).start()
                 self.low[h] = ((self.own_part * part + self.own_in * came) * (1.0 / DH)).astype(BF16)
 
         def take(self, h):

time: 73.5 us -> 67.1 us (0.913)
  Pallas kernels: 65.5 us -> 59 us
    pallas_call x1, Pallas kernels: 65.5 us -> 59 us  [shards(): pl.pallas_call(functools.partial(kernel, heads, tokens, seqs, reps, doc_l...]
where the time goes in v3:
time: 67.1 us; the launch traced here: 66.9 us
  Pallas kernels  59 us (88%)
  local copies, waits for them, and re-layouts  7.22 us (11%)
    pallas_call x1, Pallas kernels, shards(): pl.pallas_call(functools.partial(kernel, heads, tokens, seqs, reps, doc_l...  59 us
    unnamed x9, local copies, waits for them, and re-layouts  7.22 us

profile of v3, /device:TPU:0, one launch (start us, length us, event | category | flops | bytes accessed | tf_op | source)
XLA Modules:
  0.0 66.9 jit_solution(13957427540482940210)
XLA Ops:
  0.6 0.0 copy-start
  0.6 0.7 %copy-done = f32[2048]{0:T(1024)S(1)} copy-done((f32[2048]{0:T(1024)S(1)}, f32[2048]{0:T(1024)}, u32[]{:S(2)}) %copy-start) | copy-done | bytes 8216
  1.3 0.0 copy-start.1
  1.3 0.7 copy-done.1
  2.0 59.0 %shard_map.101 = (bf16[512,2048]{1,0:T(8,128)(2,1)S(1)}, bf16[512,2048]{1,0:T(8,128)(2,1)S(1)}, bf16[512,2048]{1,0:T(8,128)(2,1)S(1)}, bf16[512,2048]{1,0:T(8,128)(2,1)S(1)}, f32[16,128]{1,0:T(8,128)S(1)}) custom-call(s32[8]{0:T(128)S(1)} %copy-done.1, f32[16,128]{1,0:T(8,128)S(1)} %bitcast.2, bf16[512,2048]{1,0:T(8,128)(2,1)} %q_hbm.1, ...), custom_call_target="tpu_custom_call" | custom-call | tf_op jit(solution)/shard_map/pallas_call | solution.py:332
  61.0 1.3 %copy.16 = bf16[512,2048]{1,0:T(8,128)(2,1)} copy(bf16[512,2048]{1,0:T(8,128)(2,1)S(1)} %get-tuple-element.20) | data formatting | bytes 4194304
  62.4 1.3 %copy.17 = bf16[512,2048]{1,0:T(8,128)(2,1)} copy(bf16[512,2048]{1,0:T(8,128)(2,1)S(1)} %get-tuple-element.21) | data formatting | bytes 4194304
  63.7 1.3 %copy.18 = bf16[512,2048]{1,0:T(8,128)(2,1)} copy(bf16[512,2048]{1,0:T(8,128)(2,1)S(1)} %get-tuple-element.22) | data formatting | bytes 4194304
  65.0 1.3 %copy.19 = bf16[512,2048]{1,0:T(8,128)(2,1)} copy(bf16[512,2048]{1,0:T(8,128)(2,1)S(1)} %get-tuple-element.23) | data formatting | bytes 4194304
  66.3 0.6 copy.20
Async XLA Ops:
  0.6 0.7 %copy-start = (f32[2048]{0:T(1024)S(1)}, f32[2048]{0:T(1024)}, u32[]{:S(2)}) copy-start(f32[2048]{0:T(1024)} %param.11) | copy-start | bytes 24580
  1.3 0.7 copy-start.1
